TPU v7x, 256 devices: a whole 4x4x8 slice. The times are simulated.
256 devices in a mesh: row: 8 (over z_lo, y), col: 16 (over z_hi, x), leaf: 2 (over core).
Axes of the slice: x: 4, y: 4, z: 8 (z_hi: 4, z_lo: 2; z = z_hi * 2 + z_lo), core: 2. Of those that a mesh axis runs over, the one named last changes fastest.
Arguments:
- front: float32 [16384, 16384], P('row', ('col', 'leaf')), may hold values from -6 to 6
- child: float32 [16384, 16384], P(('row', 'col', 'leaf')), may hold values from -6 to 6
- row_map: int32 [8, 8], P('row'), may hold values from 0 to 7, each once within a row
- col_map: int32 [64], replicated, may hold values from 0 to 63, each once
- x_fac: float32 [64, 16384], P('row', ('col', 'leaf')), may hold values from -0.75 to 0.75
- w_fac: float32 [64, 16384], P('row', ('col', 'leaf')), may hold values from -0.375 to 0.375
- v_fac: float32 [64, 16384], P(('col', 'leaf'), 'row'), may hold values from -6 to 6
- z_fac: float32 [64, 16384], P(('col', 'leaf'), 'row'), may hold values from -0.75 to 0.75
- dinv: float32 [256, 256], replicated, may hold values from -0.375 to 0.375
- pivots: int32 [256], replicated, may hold values from 0 to 255, each once
- rank_rows: int32 [64], P('row'), may hold values from 16 to 64
- rank_cols: int32 [64], P(('col', 'leaf')), may hold values from 16 to 64
- admissible: int32 [64, 64], P('row', ('col', 'leaf')), may hold values 0 or 1
Outputs:
- updated: float32 [16384, 16384], P('row', ('col', 'leaf'))
Inputs may be any that keep to these rules, and one draw needn't show every extreme that they name: Each row of row_map orders the 8 tile rows of one group; col_map orders all 64 tile columns. `pivots`: A permutation of the panel's columns.
All inputs are finite; a program needn't handle non-finite values. No bound on the sum of `admissible` on one device may be relied on, other than what follows from the above.
Results may differ from a plain program's by a relative error of at most 0.0003.
Values sent between devices are 32-bit elements; how exact they have to be, the bound alone decides.
A program may use at most 128 MiB of HBM per device.

v0:
```python
import jax
import jax.numpy as jnp
from jax import lax
from jax.sharding import PartitionSpec as P

RMAX = 64


def inverse_order(order):
    count = order.shape[0]
    return jnp.zeros((count,), jnp.int32).at[order].set(jnp.arange(count, dtype=jnp.int32))


def on_device(
    front,
    child,
    row_map,
    col_map,
    x_fac,
    w_fac,
    v_fac,
    z_fac,
    dinv,
    pivots,
    rank_rows,
    rank_cols,
    admissible,
):
    highest = lax.Precision.HIGHEST
    tile = dinv.shape[0]
    row_tiles = front.shape[0] // tile
    col_tiles = front.shape[1] // tile
    col_width = front.shape[1]
    all_cols = col_map.shape[0]
    local_rows = child.shape[0]
    col_count = lax.axis_size("col")
    leaf_count = lax.axis_size("leaf")
    placed = jnp.take(child.reshape(local_rows, all_cols, tile), inverse_order(col_map), axis=1)
    outbound = placed.reshape(1, local_rows, col_count * leaf_count, col_width)
    arrived = lax.all_to_all(outbound, ("col", "leaf"), split_axis=2, concat_axis=0, tiled=True)
    grouped = arrived.reshape(row_tiles, tile, col_width)
    relaid = jnp.take(grouped, inverse_order(row_map[0]), axis=0).reshape(
        row_tiles * tile, col_width
    )
    x_whole, w_whole = (
        lax.all_gather(x_fac, ("col", "leaf"), axis=1, tiled=True),
        lax.all_gather(w_fac, ("col", "leaf"), axis=1, tiled=True),
    )
    v_whole, z_whole = (
        lax.all_gather(v_fac, "row", axis=1, tiled=True),
        lax.all_gather(z_fac, "row", axis=1, tiled=True),
    )
    x_three = x_whole.reshape(row_tiles, RMAX, tile)
    w_three = w_whole.reshape(row_tiles, RMAX, tile)
    v_three = v_whole.reshape(col_tiles, RMAX, tile)
    z_three = z_whole.reshape(col_tiles, RMAX, tile)
    dv = jnp.einsum("kb,jrb->jkr", dinv, v_three, precision=highest)
    permuted = jnp.take(w_three, pivots, axis=2)
    core = jnp.einsum("irk,jks->ijrs", permuted, dv, precision=highest)
    rank_index = jnp.arange(RMAX, dtype=jnp.int32)
    dense_tile = (admissible == 0)[:, :, None]
    keep_rows = (rank_index[None, None, :] < rank_rows[:, None, None]) | dense_tile
    keep_cols = (rank_index[None, None, :] < rank_cols[None, :, None]) | dense_tile
    core = jnp.where(keep_rows[:, :, :, None] & keep_cols[:, :, None, :], core, jnp.float32(0.0))
    left = jnp.einsum("irb,ijrs->ibjs", x_three, core, precision=highest)
    update = jnp.einsum("ibjs,jsc->ibjc", left, z_three, precision=highest).reshape(
        row_tiles * tile, col_width
    )
    return front + relaid - update


def solution(mesh):
    return jax.shard_map(
        on_device,
        mesh=mesh,
        in_specs=(
            P("row", ("col", "leaf")),
            P(("row", "col", "leaf"), None),
            P("row", None),
            P(),
            P("row", ("col", "leaf")),
            P("row", ("col", "leaf")),
            P(("col", "leaf"), "row"),
            P(("col", "leaf"), "row"),
            P(),
            P(),
            P("row"),
            P(("col", "leaf")),
            P("row", ("col", "leaf")),
        ),
        out_specs=P("row", ("col", "leaf")),
        check_vma=False,
    )
```

profile of v0, /device:TPU:1, one launch (start us, length us, event | category | flops | bytes accessed | tf_op | source)
XLA Modules:
  0.0 322.9 jit_solution(7695282449139520069)
XLA Ops:
  0.0 0.7 compare_select_fusion.2
  0.7 0.8 scatter_custom_fusion.1
  1.5 4.8 %copy.71 = f32[8,64,8,256]{3,2,0,1:T(8,128)} copy(f32[8,64,8,256]{3,2,1,0:T(8,128)} %bitcast.71) | data formatting | bytes 8388608 | tf_op jit(solution)/shard_map/reshape | solution.py:38
  6.3 4.9 %gather_fusion = f32[64,64,256]{2,1,0:T(8,128)} fusion(f32[64,64,256]{2,0,1:T(8,128)} %bitcast.69, s32[1024]{0:T(1024)S(1)} %pad_clamp_fusion.2), kind=kCustom, calls=%fused_computation | custom fusion | bytes 8388864 | tf_op jit(solution)/shard_map/jit(_take)/gather | solution.py:38
  11.3 6.6 %copy.32 = f32[64,64,256]{2,1,0:T(8,128)} copy(f32[64,64,256]{2,0,1:T(8,128)} %bitcast.67) | data formatting | bytes 8388608 | tf_op jit(solution)/shard_map/jit(_take)/gather | solution.py:38
  17.9 5.2 %gather.17 = f32[1,64,32,512]{3,2,1,0:T(8,128)} reshape(f32[64,64,256]{2,1,0:T(8,128)} %copy.32) | data formatting | bytes 8388608 | tf_op jit(solution)/shard_map/jit(_take)/gather | solution.py:38
  23.4 2.8 broadcast_select_fusion
  26.2 4.4 %copy.33 = f32[1,64,32,512]{3,1,0,2:T(8,128)} copy(f32[1,64,32,512]{3,2,1,0:T(8,128)S(1)} %broadcast_select_fusion) | data formatting | bytes 8388608 | tf_op jit(solution)/shard_map/jit(_take)/select_n | solution.py:38
  30.6 12.8 %all-to-all-start = ((f32[1,64,32,512]{3,1,0,2:T(8,128)}), f32[1,64,32,512]{3,1,0,2:T(8,128)}, u32[]{:S(2)}, u32[]{:S(2)}) async-start(f32[1,64,32,512]{3,1,0,2:T(8,128)} %copy.33), calls=%async_computation | async-start | bytes 8388608 | tf_op jit(solution)/shard_map/all_to_all | solution.py:40
  43.5 129.5 %all_gather.13 = f32[8,16384]{1,0:T(8,128)S(1)} all-gather(f32[8,512]{1,0:T(8,128)S(1)} %copy-done.2), channel_id=1, replica_groups=mesh['row'=8,'col'=16,'leaf'=2] {'col','leaf'}, dimensions={1}, use_global_device_ids=true | all-gather | bytes 540672 | tf_op jit(solution)/shard_map/all_gather | solution.py:47
  173.6 1.0 gather_fusion.2
  174.7 22.0 %all_gather.12 = f32[2,16384]{1,0:T(2,128)S(1)} all-gather(f32[2,2048]{1,0:T(2,128)S(1)} %copy-done.3), channel_id=1, replica_groups=mesh['row'=8,'col'=16,'leaf'=2] {'row'}, dimensions={1}, use_global_device_ids=true | all-gather | bytes 147456 | tf_op jit(solution)/shard_map/all_gather | solution.py:50
  196.7 21.8 %all_gather.15 = f32[2,16384]{1,0:T(2,128)S(1)} all-gather(f32[2,2048]{1,0:T(2,128)S(1)} %copy-done.4), channel_id=1, replica_groups=mesh['row'=8,'col'=16,'leaf'=2] {'row'}, dimensions={1}, use_global_device_ids=true | all-gather | bytes 147456 | tf_op jit(solution)/shard_map/all_gather | solution.py:51
  219.1 54.4 %all_gather.14 = f32[8,16384]{1,0:T(8,128)S(1)} all-gather(f32[8,512]{1,0:T(8,128)S(1)} %copy-done.5), channel_id=1, replica_groups=mesh['row'=8,'col'=16,'leaf'=2] {'col','leaf'}, dimensions={1}, use_global_device_ids=true | all-gather | bytes 540672 | tf_op jit(solution)/shard_map/all_gather | solution.py:46
  273.9 0.9 fusion
  274.8 1.1 convolution_bitcast_fusion.1
  275.9 5.0 %convolution_bitcast_fusion = f32[8,256,2,256]{3,1,0,2:T(8,128)} fusion(f32[8,256,2,64]{1,3,0,2:T(8,128)S(1)} %convolution_bitcast_fusion.1, f32[1,2,64,256]{3,1,2,0:T(2,128)S(1)} %bitcast.76), kind=kOutput, calls=%fused_computation.7 | convolution fusion | flops 805306368 | bytes 5373952 | tf_op jit(solution)/shard_map/ibjs,jsc->ibjc/dot_general | solution.py:66
  280.9 5.5 %copy.40 = f32[8,256,2,256]{1,0,3,2:T(8,128)} copy(f32[8,256,2,256]{3,1,0,2:T(8,128)} %convolution_bitcast_fusion) | data formatting | bytes 8388608 | tf_op jit(solution)/shard_map/ibjs,jsc->ibjc/transpose | solution.py:66
  286.4 6.2 %copy.52 = f32[64,8,8,256]{3,1,2,0:T(8,128)} copy(f32[64,8,8,256]{3,2,1,0:T(8,128)} %bitcast.70) | data formatting | bytes 8388608
  293.3 5.4 %copy.35 = f32[2048,512]{0,1:T(8,128)} copy(f32[2048,512]{1,0:T(8,128)} %param.13) | data formatting | bytes 8388608 | tf_op args[0]
  298.7 5.0 %gather_fusion.1 = f32[8,256,512]{2,1,0:T(8,128)} fusion(f32[8,256,512]{2,1,0:T(8,128)} %bitcast.5, s32[1024]{0:T(1024)S(1)} %pad_clamp_fusion.1), kind=kCustom, calls=%fused_computation.1 | custom fusion | bytes 8388640 | tf_op jit(solution)/shard_map/jit(_take)/gather | solution.py:42
  303.7 5.4 %copy.34 = f32[2048,512]{0,1:T(8,128)} copy(f32[2048,512]{1,0:T(8,128)} %bitcast.68) | data formatting | bytes 8388608 | tf_op jit(solution)/shard_map/jit(_take)/gather | solution.py:42
  309.1 8.5 %add_subtract_fusion = f32[2048,512]{0,1:T(8,128)} fusion(f32[2048,512]{0,1:T(8,128)} %bitcast.66, f32[2048,512]{0,1:T(8,128)} %copy.35, f32[2048,512]{0,1:T(8,128)} %copy.34, pred[2048]{0:T(1024)(128)(4,1)S(1)} %broadcast_in_dim.62), kind=kLoop, calls=%fused_computation.6 | loop fusion | flops 3145728 | bytes 16779264 | tf_op jit(solution)/shard_map/sub | solution.py:69
  317.5 5.3 %copy.41 = f32[2048,512]{1,0:T(8,128)} copy(f32[2048,512]{0,1:T(8,128)} %add_subtract_fusion) | data formatting | bytes 8388608 | tf_op jit(solution)/shard_map/sub | solution.py:69
  (50 shorter events, 2.7 us)
Async XLA Ops:
  0.0 218.5 %copy-start = (f32[256,256]{1,0:T(8,128)S(1)}, f32[256,256]{1,0:T(8,128)}, u32[]{:S(2)}) copy-start(f32[256,256]{1,0:T(8,128)} %param.21) | copy-start | bytes 786436
  30.6 12.8 %copy-start.7 = (s32[8,2]{0,1:T(2,128)S(1)}, s32[8,2]{0,1:T(2,128)}, u32[]{:S(2)}) copy-start(s32[8,2]{0,1:T(2,128)} %param.25) | copy-start | bytes 196
  30.6 13.0 %copy-start.2 = (f32[8,512]{1,0:T(8,128)S(1)}, f32[8,512]{1,0:T(8,128)}, u32[]{:S(2)}) copy-start(f32[8,512]{1,0:T(8,128)} %param.18) | copy-start | bytes 49156
  30.6 143.0 %copy-start.6 = (s32[256]{0:T(256)S(1)}, s32[256]{0:T(256)}, u32[]{:S(2)}) copy-start(s32[256]{0:T(256)} %param.22) | copy-start | bytes 3076
  30.6 268.2 %all-to-all-start = ((f32[1,64,32,512]{3,1,0,2:T(8,128)}), f32[1,64,32,512]{3,1,0,2:T(8,128)}, u32[]{:S(2)}, u32[]{:S(2)}) async-start(f32[1,64,32,512]{3,1,0,2:T(8,128)} %copy.33), calls=%async_computation | async-start | bytes 8388608 | tf_op jit(solution)/shard_map/all_to_all | solution.py:40
  43.4 131.3 %copy-start.3 = (f32[2,2048]{1,0:T(2,128)S(1)}, f32[2,2048]{1,0:T(2,128)}, u32[]{:S(2)}) copy-start(f32[2,2048]{1,0:T(2,128)} %param.19) | copy-start | bytes 49156
  43.4 153.3 %copy-start.4 = (f32[2,2048]{1,0:T(2,128)S(1)}, f32[2,2048]{1,0:T(2,128)}, u32[]{:S(2)}) copy-start(f32[2,2048]{1,0:T(2,128)} %param.20) | copy-start | bytes 49156
  43.4 175.5 %copy-start.8 = (s32[2]{0:T(128)S(1)}, s32[2]{0:T(128)}, u32[]{:S(2)}) copy-start(s32[2]{0:T(128)} %param.24) | copy-start | bytes 28
  43.4 175.6 %copy-start.9 = (s32[8]{0:T(128)S(1)}, s32[8]{0:T(128)}, u32[]{:S(2)}) copy-start(s32[8]{0:T(128)} %param.23) | copy-start | bytes 100
  43.4 175.7 %copy-start.5 = (f32[8,512]{1,0:T(8,128)S(1)}, f32[8,512]{1,0:T(8,128)}, u32[]{:S(2)}) copy-start(f32[8,512]{1,0:T(8,128)} %param.17) | copy-start | bytes 49156
  286.4 6.2 %copy-start.10 = (s32[1,8]{1,0:T(1,128)S(1)}, s32[1,8]{1,0:T(1,128)}, u32[]{:S(2)}) copy-start(s32[1,8]{1,0:T(1,128)} %param.15) | copy-start | bytes 100
  309.1 13.8 %copy-start.1 = (f32[256,256]{1,0:T(8,128)S(1)}, f32[256,256]{1,0:T(8,128)}, u32[]{:S(2)}) copy-start(f32[256,256]{1,0:T(8,128)} %param.21) | copy-start | bytes 786436
where the time goes:
time: 324 us; the launch traced here: 323 us
  blocking collectives  228 us (70%)
  local copies, waits for them, and re-layouts  62.2 us (19%)
  starting transfers between devices  12.8 us (4%)
  other arithmetic  12.6 us (4%)
  matrix products  7.41 us (2%)
    all_gather x1, blocking collectives, on_device(): lax.all_gather(w_fac, ('col', 'leaf'), axis=1, tiled=True)  129 us
    all_gather x1, blocking collectives, on_device(): lax.all_gather(x_fac, ('col', 'leaf'), axis=1, tiled=True)  54.4 us
    all_gather x1, blocking collectives, on_device(): lax.all_gather(v_fac, 'row', axis=1, tiled=True)  22 us
    all_gather x1, blocking collectives, on_device(): lax.all_gather(z_fac, 'row', axis=1, tiled=True)  21.8 us
    gather x3, local copies, waits for them, and re-layouts, on_device(): jnp.take(child.reshape(local_rows, all_cols, tile), inverse_order(col_map...  16.8 us
    all_to_all x1, starting transfers between devices, on_device(): lax.all_to_all(outbound, ('col', 'leaf'), split_axis=2, concat_axis=0, ti...  12.8 us
    unnamed x26, local copies, waits for them, and re-layouts  11.8 us
    gather x2, local copies, waits for them, and re-layouts, on_device(): jnp.take(grouped, inverse_order(row_map[0]), axis=0)  10.3 us
  transfers between devices with their start and end apart: 1, of which 0 were waited for; matrix products, arithmetic and copies ran while one was open for 9% of the time, Pallas kernels for 0%

commit v1 on v0

--- a/solution.py
+++ b/solution.py
@@ -44,7 +44,12 @@
     )
     x_whole, w_whole = (
         lax.all_gather(x_fac, ("col", "leaf"), axis=1, tiled=True),
-        lax.all_gather(w_fac, ("col", "leaf"), axis=1, tiled=True),
+        jnp.concatenate(
+            lax.all_to_all(
+                jnp.stack([w_fac] * lax.axis_size(("col", "leaf"))), ("col", "leaf"), 0, 0
+            ),
+            axis=1,
+        ),
     )
     v_whole, z_whole = (
         lax.all_gather(v_fac, "row", axis=1, tiled=True),

time: 324 us -> 292 us (0.901)
  blocking collectives: 228 us -> 185 us
  starting transfers between devices: 12.8 us -> 22.6 us
    all_gather x1 -> x0, blocking collectives: 129 us -> none  [on_device(): lax.all_gather(w_fac, ('col', 'leaf'), axis=1, tiled=True)]
    all_gather x1, blocking collectives: 22 us -> 103 us  [on_device(): lax.all_gather(v_fac, 'row', axis=1, tiled=True)]
    all_to_all x0 -> x1, starting transfers between devices: none -> 12.6 us  [on_device(): lax.all_to_all(jnp.stack([w_fac] * lax.axis_size(('col', 'leaf'))), ('col...]
    all_gather x1, blocking collectives: 54.4 us -> 59.9 us  [on_device(): lax.all_gather(x_fac, ('col', 'leaf'), axis=1, tiled=True)]
    unnamed x26 -> x23, local copies, waits for them, and re-layouts: 11.8 us -> 11.6 us
  transfers between devices with their start and end apart: 1 -> 2, of which waited for: 0 -> 0; matrix products, arithmetic and copies ran while one was open for 9% -> 20% of each run, Pallas kernels for 0% -> 0%
where the time goes in v1:
time: 292 us
  blocking collectives  185 us (63%)
  local copies, waits for them, and re-layouts  64 us (22%)
  starting transfers between devices  22.6 us (8%)
  other arithmetic  12.5 us (4%)
  matrix products  7.42 us (3%)
    all_gather x1, blocking collectives, on_device(): lax.all_gather(v_fac, 'row', axis=1, tiled=True)  103 us
    all_gather x1, blocking collectives, on_device(): lax.all_gather(x_fac, ('col', 'leaf'), axis=1, tiled=True)  59.9 us
    all_gather x1, blocking collectives, on_device(): lax.all_gather(z_fac, 'row', axis=1, tiled=True)  21.8 us
    gather x3, local copies, waits for them, and re-layouts, on_device(): jnp.take(child.reshape(local_rows, all_cols, tile), inverse_order(col_map...  16.8 us
    all_to_all x1, starting transfers between devices, on_device(): lax.all_to_all(jnp.stack([w_fac] * lax.axis_size(('col', 'leaf'))), ('col...  12.6 us
    unnamed x23, local copies, waits for them, and re-layouts  11.6 us
    gather x2, local copies, waits for them, and re-layouts, on_device(): jnp.take(grouped, inverse_order(row_map[0]), axis=0)  10.4 us
    all_to_all x1, starting transfers between devices, on_device(): lax.all_to_all(outbound, ('col', 'leaf'), split_axis=2, concat_axis=0, ti...  9.97 us
  transfers between devices with their start and end apart: 2, of which 0 were waited for; matrix products, arithmetic and copies ran while one was open for 20% of the time, Pallas kernels for 0%

profile of v1, /device:TPU:1, one launch (start us, length us, event | category | flops | bytes accessed | tf_op | source)
XLA Modules:
  0.0 291.6 jit_solution(5892506172598094769)
XLA Ops:
  0.0 1.6 stack.2
  1.6 12.6 %all-to-all-start.1 = ((f32[32,8,512]{2,1,0:T(8,128)}), f32[32,8,512]{2,1,0:T(8,128)S(1)}, u32[]{:S(2)}, u32[]{:S(2)}) async-start(f32[32,8,512]{2,1,0:T(8,128)} %stack.2), calls=%async_computation.1 | async-start | bytes 1048576 | tf_op jit(solution)/shard_map/all_to_all | solution.py:48
  14.9 4.8 %copy.71 = f32[8,64,8,256]{3,2,0,1:T(8,128)} copy(f32[8,64,8,256]{3,2,1,0:T(8,128)} %bitcast.68) | data formatting | bytes 8388608 | tf_op jit(solution)/shard_map/reshape | solution.py:38
  19.7 0.8 scatter_custom_fusion.1
  20.5 5.0 %gather_fusion = f32[64,64,256]{2,1,0:T(8,128)} fusion(f32[64,64,256]{2,0,1:T(8,128)} %bitcast.64, s32[1024]{0:T(1024)S(1)} %pad_clamp_fusion.2), kind=kCustom, calls=%fused_computation | custom fusion | bytes 8388864 | tf_op jit(solution)/shard_map/jit(_take)/gather | solution.py:38
  25.5 6.6 %copy.33 = f32[64,64,256]{2,1,0:T(8,128)} copy(f32[64,64,256]{2,0,1:T(8,128)} %bitcast.65) | data formatting | bytes 8388608 | tf_op jit(solution)/shard_map/jit(_take)/gather | solution.py:38
  32.1 5.2 %gather.17 = f32[1,64,32,512]{3,2,1,0:T(8,128)} reshape(f32[64,64,256]{2,1,0:T(8,128)} %copy.33) | data formatting | bytes 8388608 | tf_op jit(solution)/shard_map/jit(_take)/gather | solution.py:38
  37.6 2.8 broadcast_select_fusion
  40.3 4.4 %copy.34 = f32[1,64,32,512]{3,1,0,2:T(8,128)} copy(f32[1,64,32,512]{3,2,1,0:T(8,128)S(1)} %broadcast_select_fusion) | data formatting | bytes 8388608 | tf_op jit(solution)/shard_map/jit(_take)/select_n | solution.py:38
  44.7 10.0 %all-to-all-start = ((f32[1,64,32,512]{3,1,0,2:T(8,128)}), f32[1,64,32,512]{3,1,0,2:T(8,128)}, u32[]{:S(2)}, u32[]{:S(2)}) async-start(f32[1,64,32,512]{3,1,0,2:T(8,128)} %copy.34), calls=%async_computation | async-start | bytes 8388608 | tf_op jit(solution)/shard_map/all_to_all | solution.py:40
  55.6 5.4 %copy.36 = f32[2048,512]{0,1:T(8,128)} copy(f32[2048,512]{1,0:T(8,128)} %param.13) | data formatting | bytes 8388608 | tf_op args[0]
  61.1 103.1 %all_gather.9 = f32[2,16384]{1,0:T(2,128)S(1)} all-gather(f32[2,2048]{1,0:T(2,128)S(1)} %copy-done.2), channel_id=1, replica_groups=mesh['row'=8,'col'=16,'leaf'=2] {'row'}, dimensions={1}, use_global_device_ids=true | all-gather | bytes 147456 | tf_op jit(solution)/shard_map/all_gather | solution.py:55
  164.2 21.8 %all_gather.11 = f32[2,16384]{1,0:T(2,128)S(1)} all-gather(f32[2,2048]{1,0:T(2,128)S(1)} %copy-done.3), channel_id=1, replica_groups=mesh['row'=8,'col'=16,'leaf'=2] {'row'}, dimensions={1}, use_global_device_ids=true | all-gather | bytes 147456 | tf_op jit(solution)/shard_map/all_gather | solution.py:56
  186.7 59.9 %all_gather.10 = f32[8,16384]{1,0:T(8,128)S(1)} all-gather(f32[8,512]{1,0:T(8,128)S(1)} %copy-done.4), channel_id=1, replica_groups=mesh['row'=8,'col'=16,'leaf'=2] {'col','leaf'}, dimensions={1}, use_global_device_ids=true | all-gather | bytes 540672 | tf_op jit(solution)/shard_map/all_gather | solution.py:46
  247.4 1.0 gather_fusion.2
  248.8 0.9 fusion
  249.7 1.1 convolution_bitcast_fusion.1
  250.8 5.0 %convolution_bitcast_fusion = f32[8,256,2,256]{3,1,0,2:T(8,128)} fusion(f32[8,256,2,64]{1,3,0,2:T(8,128)S(1)} %convolution_bitcast_fusion.1, f32[1,2,64,256]{3,1,2,0:T(2,128)S(1)} %bitcast.72), kind=kOutput, calls=%fused_computation.7 | convolution fusion | flops 805306368 | bytes 5373952 | tf_op jit(solution)/shard_map/ibjs,jsc->ibjc/dot_general | solution.py:71
  255.8 5.4 %copy.42 = f32[8,256,2,256]{1,0,3,2:T(8,128)} copy(f32[8,256,2,256]{3,1,0,2:T(8,128)} %convolution_bitcast_fusion) | data formatting | bytes 8388608 | tf_op jit(solution)/shard_map/ibjs,jsc->ibjc/transpose | solution.py:71
  261.3 6.2 %copy.53 = f32[64,8,8,256]{3,1,2,0:T(8,128)} copy(f32[64,8,8,256]{3,2,1,0:T(8,128)} %bitcast.67) | data formatting | bytes 8388608
  267.4 5.0 %gather_fusion.1 = f32[8,256,512]{2,1,0:T(8,128)} fusion(f32[8,256,512]{2,1,0:T(8,128)} %bitcast.5, s32[1024]{0:T(1024)S(1)} %pad_clamp_fusion.1), kind=kCustom, calls=%fused_computation.1 | custom fusion | bytes 8388640 | tf_op jit(solution)/shard_map/jit(_take)/gather | solution.py:42
  272.4 5.4 %copy.35 = f32[2048,512]{0,1:T(8,128)} copy(f32[2048,512]{1,0:T(8,128)} %bitcast.66) | data formatting | bytes 8388608 | tf_op jit(solution)/shard_map/jit(_take)/gather | solution.py:42
  277.8 8.4 %add_subtract_fusion = f32[2048,512]{0,1:T(8,128)} fusion(f32[2048,512]{0,1:T(8,128)} %bitcast.63, f32[2048,512]{0,1:T(8,128)} %copy.36, f32[2048,512]{0,1:T(8,128)} %copy.35, pred[2048]{0:T(1024)(128)(4,1)S(1)} %broadcast_in_dim.62), kind=kLoop, calls=%fused_computation.6 | loop fusion | flops 3145728 | bytes 16779264 | tf_op jit(solution)/shard_map/sub | solution.py:74
  286.3 5.3 %copy.43 = f32[2048,512]{1,0:T(8,128)} copy(f32[2048,512]{0,1:T(8,128)} %add_subtract_fusion) | data formatting | bytes 8388608 | tf_op jit(solution)/shard_map/sub | solution.py:74
  (51 shorter events, 3.6 us)
Async XLA Ops:
  0.0 186.0 %copy-start = (f32[256,256]{1,0:T(8,128)S(1)}, f32[256,256]{1,0:T(8,128)}, u32[]{:S(2)}) copy-start(f32[256,256]{1,0:T(8,128)} %param.21) | copy-start | bytes 786436
  1.6 43.1 %all-to-all-start.1 = ((f32[32,8,512]{2,1,0:T(8,128)}), f32[32,8,512]{2,1,0:T(8,128)S(1)}, u32[]{:S(2)}, u32[]{:S(2)}) async-start(f32[32,8,512]{2,1,0:T(8,128)} %stack.2), calls=%async_computation.1 | async-start | bytes 1048576 | tf_op jit(solution)/shard_map/all_to_all | solution.py:48
  44.7 10.0 %copy-start.6 = (s32[8,2]{0,1:T(2,128)S(1)}, s32[8,2]{0,1:T(2,128)}, u32[]{:S(2)}) copy-start(s32[8,2]{0,1:T(2,128)} %param.25) | copy-start | bytes 196
  44.7 10.1 %copy-start.7 = (s32[1,8]{1,0:T(1,128)S(1)}, s32[1,8]{1,0:T(1,128)}, u32[]{:S(2)}) copy-start(s32[1,8]{1,0:T(1,128)} %param.15) | copy-start | bytes 100
  44.7 222.7 %all-to-all-start = ((f32[1,64,32,512]{3,1,0,2:T(8,128)}), f32[1,64,32,512]{3,1,0,2:T(8,128)}, u32[]{:S(2)}, u32[]{:S(2)}) async-start(f32[1,64,32,512]{3,1,0,2:T(8,128)} %copy.34), calls=%async_computation | async-start | bytes 8388608 | tf_op jit(solution)/shard_map/all_to_all | solution.py:40
  55.6 5.5 %copy-start.2 = (f32[2,2048]{1,0:T(2,128)S(1)}, f32[2,2048]{1,0:T(2,128)}, u32[]{:S(2)}) copy-start(f32[2,2048]{1,0:T(2,128)} %param.19) | copy-start | bytes 49156
  55.6 108.6 %copy-start.3 = (f32[2,2048]{1,0:T(2,128)S(1)}, f32[2,2048]{1,0:T(2,128)}, u32[]{:S(2)}) copy-start(f32[2,2048]{1,0:T(2,128)} %param.20) | copy-start | bytes 49156
  55.6 130.4 %copy-start.5 = (s32[256]{0:T(256)S(1)}, s32[256]{0:T(256)}, u32[]{:S(2)}) copy-start(s32[256]{0:T(256)} %param.22) | copy-start | bytes 3076
  55.6 130.8 %copy-start.8 = (s32[2]{0:T(128)S(1)}, s32[2]{0:T(128)}, u32[]{:S(2)}) copy-start(s32[2]{0:T(128)} %param.24) | copy-start | bytes 28
  55.6 130.9 %copy-start.9 = (s32[8]{0:T(128)S(1)}, s32[8]{0:T(128)}, u32[]{:S(2)}) copy-start(s32[8]{0:T(128)} %param.23) | copy-start | bytes 100
  55.6 131.1 %copy-start.4 = (f32[8,512]{1,0:T(8,128)S(1)}, f32[8,512]{1,0:T(8,128)}, u32[]{:S(2)}) copy-start(f32[8,512]{1,0:T(8,128)} %param.17) | copy-start | bytes 49156
  277.8 13.8 %copy-start.1 = (f32[256,256]{1,0:T(8,128)S(1)}, f32[256,256]{1,0:T(8,128)}, u32[]{:S(2)}) copy-start(f32[256,256]{1,0:T(8,128)} %param.21) | copy-start | bytes 786436
